TPU v7x, 32 devices: a whole 2x2x4 slice. The times are simulated.
32 devices in a mesh: groups: 2 (over x), dp: 16 (over z, y, core).
Axes of the slice: x: 2, y: 2, z: 4, core: 2. Of those that a mesh axis runs over, the one named last changes fastest.
Arguments:
- activations: bfloat16 [12288, 16384], P(('groups', 'dp')), parts along dimension 0, may hold values from -18 to 18
- labels: int32 [12288], P(('groups', 'dp')), parts along dimension 0, may hold values from 0 to 63, as said below
- counts: int32 [12288], P(('groups', 'dp')), parts along dimension 0, may hold values from 1 to 4
Outputs:
- solution: float32 [32768, 64], P(('groups', 'dp')), parts along dimension 0
- residual: float32 [32768, 64], P(('groups', 'dp')), parts along dimension 0
There are 2 independent parts, one for each index of `groups`. A program takes and returns all parts, laid end to end along the dimension named above; each array names one. Nothing has to cross between parts.
Inputs may be any that keep to these rules, and one draw needn't show every extreme that they name: `labels`: concept index of each row; every concept of 0 to 63 names at least one row. `counts`: integer sample weight of each row.
All inputs are finite; a program needn't handle non-finite values.
Results may differ from a plain program's by a relative error of at most 0.012.
The roundings to bfloat16 on the way count: a program that leaves them out, or rounds other values in their place, can miss the bound.
Values may be sent and summed in bfloat16 or wider, within the bound.
No kernel may reach another device: no remote copies, remote signals or barrier semaphores. Data moves between devices by JAX's collectives and lax.ppermute only.
A program may use at most 64 MiB of HBM per device.

v0:
```python
import jax
import jax.numpy as jnp
from jax import lax
from jax.sharding import PartitionSpec as P

K = 64
ITERS = 2
RIDGE = 0.1


def precise(left_side, right_side):
    return jnp.dot(
        left_side, right_side, precision=lax.Precision.HIGHEST, preferred_element_type=jnp.float32
    )


def symmetric(matrix):
    return 0.5 * (matrix + matrix.T)


def solve_positive(matrix, target):
    return jax.scipy.linalg.cho_solve((jnp.linalg.cholesky(matrix), True), target)


def contract_rows(left_side, right_side):
    return lax.dot_general(
        left_side, right_side, (((0,), (0,)), ((), ())), preferred_element_type=jnp.float32
    )


def per_device(activations, labels, counts):
    weights = counts.astype(jnp.float32)
    classes = jnp.arange(K, dtype=jnp.int32)
    member_full = jnp.where(labels[:, None] == classes[None, :], weights[:, None], jnp.float32(0.0))
    local_weight = jnp.sum(member_full, axis=0)
    member = member_full.astype(jnp.bfloat16)
    class_sums = lax.psum_scatter(
        contract_rows(activations, member), "dp", scatter_dimension=0, tiled=True
    )
    class_weight = lax.psum(local_weight, "dp")
    total_weight = jnp.sum(class_weight)
    class_means = class_sums / class_weight[None, :]
    mean_diff = class_means * jnp.sqrt(class_weight)[None, :]
    solution = jnp.zeros_like(mean_diff)
    residual = mean_diff
    direction = mean_diff
    current = symmetric(lax.psum(precise(residual.T, residual), "dp"))
    for iteration in range(ITERS):
        probed = jnp.dot(
            activations,
            lax.all_gather(direction.astype(jnp.bfloat16), "dp", axis=0, tiled=True),
            preferred_element_type=jnp.float32,
        )
        weighted = (weights[:, None] * probed).astype(jnp.bfloat16)
        panel = lax.psum_scatter(
            contract_rows(activations, weighted), "dp", scatter_dimension=0, tiled=True
        )
        cross, along_panel, along_along = lax.psum(
            (
                precise(class_means.T, direction),
                precise(direction.T, panel),
                precise(direction.T, direction),
            ),
            "dp",
        )
        scaled = class_weight[:, None] * cross
        curvature = symmetric(
            (along_panel - precise(cross.T, scaled)) / total_weight + RIDGE * along_along
        )
        step_alpha = solve_positive(curvature, current)
        image = (panel - precise(class_means, scaled)) / total_weight + RIDGE * direction
        solution = solution + precise(direction, step_alpha)
        residual = residual - precise(image, step_alpha)
        renewed = current
        if iteration + 1 < ITERS:
            renewed = symmetric(lax.psum(precise(residual.T, residual), "dp"))
        if iteration + 1 < ITERS:
            step_beta = solve_positive(current, renewed)
            direction = residual + precise(direction, step_beta)
            current = renewed
    return (solution, residual)


def solution(mesh):
    in_specs = (P(("groups", "dp"), None), P(("groups", "dp")), P(("groups", "dp")))
    out_specs = (P(("groups", "dp"), None), P(("groups", "dp"), None))
    return jax.shard_map(
        per_device, mesh=mesh, in_specs=in_specs, out_specs=out_specs, check_vma=False
    )
```

profile of v0, /device:TPU:0, one launch (start us, length us, event | category | flops | bytes accessed | tf_op | source)
XLA Modules:
  0.0 587.8 jit_solution(6999212861251710433)
XLA Ops:
  7.2 0.0 reduce-scatter.4.cloned.1.call-start
  7.2 0.7 convert_element_type.20
  7.9 8.9 %convolution_bitcast_fusion.2 = f32[16384,64]{0,1:T(8,128)} fusion(bf16[384,16384]{1,0:T(8,128)(2,1)} %param.6, f32[384]{0:T(512)S(1)} %convert_element_type.20, s32[384]{0:T(512)} %param.7), kind=kOutput, calls=%fused_computation.2 | convolution fusion | flops 805355520 | bytes 16780288 | tf_op jit(solution)/shard_map/dot_general | solution.py:26
  16.8 0.0 all-gather.3.cloned.1.call-start
  16.8 0.1 select_reduce_fusion
  17.0 35.0 %psum.59 = f32[64]{0:T(128)S(1)} all-reduce(f32[64]{0:T(128)S(1)} %select_reduce_fusion), channel_id=1, replica_groups=mesh['groups'=2,'dp'=16] {'dp'}, use_global_device_ids=true, to_apply=%region_2.3 | all-reduce | flops 64 | bytes 512 | tf_op jit(solution)/shard_map/psum | solution.py:40
  52.0 0.6 fusion.62
  52.6 39.5 %reduce-scatter.4.cloned.1.call-done = f32[1024,64]{0,1:T(8,128)} async-done(((f32[16384,64]{0,1:T(8,128)}), f32[1024,64]{0,1:T(8,128)}) %reduce-scatter.4.cloned.1.call-update) | async-done | bytes 262160 | tf_op jit(solution)/shard_map/reduce_scatter | solution.py:37
  92.1 1.7 multiply_convert_fusion
  93.8 0.0 reduce-scatter.6.cloned.1.call-start
  93.9 41.7 %all-gather.3.cloned.1.call-done = bf16[16384,64]{0,1:T(8,128)(2,1)} async-done(((bf16[1024,64]{0,1:T(8,128)(2,1)}), bf16[16384,64]{0,1:T(8,128)(2,1)}) %all-gather.3.cloned.1.call-update) | async-done | bytes 2097168 | tf_op jit(solution)/shard_map/all_gather | solution.py:51
  135.5 18.5 %convolution_bitcast_fusion.1 = f32[16384,64]{0,1:T(8,128)} fusion(bf16[384,16384]{1,0:T(8,128)(2,1)} %param.6, bf16[16384,64]{0,1:T(8,128)(2,1)} %all-gather.3.cloned.1.call-done, f32[384]{0:T(512)S(1)} %convert_element_type.20), kind=kOutput, calls=%fused_computation.1 | convolution fusion | flops 1610661888 | bytes 18875904 | tf_op jit(solution)/shard_map/dot_general | solution.py:26
  154.0 0.0 all-gather.5.cloned.1.call-start
  154.1 0.5 fusion.13
  154.5 0.5 fusion.15
  155.0 70.3 %reduce-scatter.6.cloned.1.call-done = f32[1024,64]{0,1:T(8,128)} async-done(((f32[16384,64]{0,1:T(8,128)}), f32[1024,64]{0,1:T(8,128)}) %reduce-scatter.6.cloned.1.call-update) | async-done | bytes 262160 | tf_op jit(solution)/shard_map/reduce_scatter | solution.py:55
  225.3 1.4 fusion.17
  226.7 59.2 %all-reduce.1 = (f32[64,64]{1,0:T(8,128)S(1)}, f32[64,64]{1,0:T(8,128)S(1)}, f32[64,64]{1,0:T(8,128)S(1)}) all-reduce(f32[64,64]{1,0:T(8,128)S(1)} %fusion.13, f32[64,64]{1,0:T(8,128)S(1)} %fusion.17, f32[64,64]{1,0:T(8,128)S(1)} %fusion.15), channel_id=1, replica_groups=mesh['groups'=2,'dp'=16] {'dp'}, use_global_device_ids=true, to_apply=%region_7.8 | all-reduce | flops 12288 | bytes 98304 | tf_op jit(solution)/shard_map/psum | solution.py:58
  285.9 0.1 copy.19
  286.0 0.1 copy.20
  286.1 5.8 cholesky.70
  292.0 0.6 compare_reduce_fusion.1
  292.6 0.7 fusion.32
  293.3 4.9 custom-call.10
  298.2 0.9 fusion.9
  299.1 0.1 copy.15
  299.2 0.1 copy.17
  299.3 0.1 copy.18
  299.4 5.9 cholesky.59
  305.3 0.6 compare_reduce_fusion.2
  305.9 0.7 fusion.31
  306.6 4.9 custom-call.9
  311.5 0.2 fusion.48
  311.7 0.2 fusion.46
  311.9 2.1 fusion.3
  314.0 0.4 convolution_subtract_fusion.2
  314.4 0.4 fusion.64
  314.8 57.6 %psum.63 = f32[64,64]{1,0:T(8,128)S(1)} all-reduce(f32[64,64]{1,0:T(8,128)S(1)} %fusion.64), channel_id=1, replica_groups=mesh['groups'=2,'dp'=16] {'dp'}, use_global_device_ids=true, to_apply=%region_10.13 | all-reduce | flops 4096 | bytes 32768 | tf_op jit(solution)/shard_map/psum | solution.py:76
  372.4 0.1 copy.21
  372.5 0.2 fusion.42
  372.8 0.2 fusion.40
  372.9 1.1 fusion.63
  374.1 0.3 reduce-scatter.8.cloned.1.call-start
  374.3 38.6 %all-gather.5.cloned.1.call-done = bf16[16384,64]{0,1:T(8,128)(2,1)} async-done(((bf16[1024,64]{0,1:T(8,128)(2,1)}), bf16[16384,64]{0,1:T(8,128)(2,1)}) %all-gather.5.cloned.1.call-update) | async-done | bytes 2097168 | tf_op jit(solution)/shard_map/all_gather | solution.py:51
  412.9 18.5 %convolution_bitcast_fusion = f32[16384,64]{0,1:T(8,128)} fusion(bf16[384,16384]{1,0:T(8,128)(2,1)} %param.6, bf16[16384,64]{0,1:T(8,128)(2,1)} %all-gather.5.cloned.1.call-done, f32[384]{0:T(512)S(1)} %convert_element_type.20), kind=kOutput, calls=%fused_computation | convolution fusion | flops 1610661888 | bytes 18875904 | tf_op jit(solution)/shard_map/dot_general | solution.py:26
  431.4 0.4 fusion.66
  431.7 0.4 fusion.61
  432.2 0.5 fusion.11
  432.6 70.1 %reduce-scatter.8.cloned.1.call-done = f32[1024,64]{0,1:T(8,128)} async-done(((f32[16384,64]{0,1:T(8,128)}), f32[1024,64]{0,1:T(8,128)}) %reduce-scatter.8.cloned.1.call-update) | async-done | bytes 262160 | tf_op jit(solution)/shard_map/reduce_scatter | solution.py:55
  502.8 1.3 fusion.65
  504.1 59.1 %all-reduce = (f32[64,64]{1,0:T(8,128)S(1)}, f32[64,64]{1,0:T(8,128)S(1)}, f32[64,64]{1,0:T(8,128)S(1)}) all-reduce(f32[64,64]{1,0:T(8,128)S(1)} %fusion.65, f32[64,64]{1,0:T(8,128)S(1)} %fusion.61, f32[64,64]{1,0:T(8,128)S(1)} %fusion.66), channel_id=1, replica_groups=mesh['groups'=2,'dp'=16] {'dp'}, use_global_device_ids=true, to_apply=%region_12.15 | all-reduce | flops 12288 | bytes 98304 | tf_op jit(solution)/shard_map/psum | solution.py:58
  563.2 0.9 fusion.7
  564.1 0.1 copy.22
  564.2 0.1 copy.23
  564.3 0.1 copy.24
  564.4 5.8 cholesky.81
  570.3 0.6 compare_reduce_fusion
  570.9 0.7 fusion.33
  571.6 4.9 custom-call.11
  576.5 0.2 fusion.36
  576.7 0.2 fusion.34
  576.9 2.1 fusion.1
  579.0 1.1 convolution_subtract_fusion
  580.1 1.1 convolution_add_fusion
  (19 shorter events, 0.3 us)
Async XLA Ops:
  7.2 9.7 %copy-start.1 = (s32[384]{0:T(512)S(1)}, s32[384]{0:T(512)}, u32[]{:S(2)}) copy-start(s32[384]{0:T(512)} %param.7) | copy-start | bytes 4612
  7.2 84.9 %reduce-scatter.4.cloned.1.call-start = ((), (), s32[]{:S(2)}) async-start(), calls=%async_computation.3 | async-start | bytes 4456448 | tf_op jit(solution)/shard_map/reduce_scatter | solution.py:37
  16.8 118.7 %all-gather.3.cloned.1.call-start = ((), (), s32[]{:S(2)}) async-start(), calls=%async_computation.4 | async-start | bytes 2228224 | tf_op jit(solution)/shard_map/all_gather | solution.py:51
  93.8 60.3 %copy-start = (f32[1024,64]{0,1:T(8,128)S(1)}, f32[1024,64]{0,1:T(8,128)}, u32[]{:S(2)}) copy-start(f32[1024,64]{0,1:T(8,128)} %reduce-scatter.4.cloned.1.call-done) | copy-start | bytes 786436
  93.8 131.5 %reduce-scatter.6.cloned.1.call-start = ((), (), s32[]{:S(2)}) async-start(), calls=%async_computation.5 | async-start | bytes 4456448 | tf_op jit(solution)/shard_map/reduce_scatter | solution.py:55
  154.0 258.9 %all-gather.5.cloned.1.call-start = ((), (), s32[]{:S(2)}) async-start(), calls=%async_computation.6 | async-start | bytes 2228224 | tf_op jit(solution)/shard_map/all_gather | solution.py:51
  374.1 128.7 %reduce-scatter.8.cloned.1.call-start = ((), (), s32[]{:S(2)}) async-start(), calls=%async_computation.7 | async-start | bytes 4456448 | tf_op jit(solution)/shard_map/reduce_scatter | solution.py:55
Sparse Core Ops, SparseCore 0:
  16.9 75.1 reduce-scatter.3
  95.1 40.4 all-gather.2
  154.1 71.1 reduce-scatter.5
  374.2 38.6 all-gather.4
  431.5 71.2 reduce-scatter.7
where the time goes:
time: 588 us
  waiting for transfers between devices  260 us (44%)
  blocking collectives  211 us (36%)
  matrix products  62 us (11%)
  other arithmetic  39.4 us (7%)
  between operations  14.1 us (2%)
    reduce_scatter x2, waiting for transfers between devices, per_device(): lax.psum_scatter(contract_rows(activations, weighted), 'dp', scatter_dime...  140 us
    psum x2, blocking collectives, per_device(): lax.psum((precise(class_means.T, direction), precise(direction.T, panel),...  118 us
    all_gather x2, waiting for transfers between devices, per_device(): lax.all_gather(direction.astype(jnp.bfloat16), 'dp', axis=0, tiled=True)  80.2 us
    psum x1, blocking collectives, per_device(): renewed = symmetric(lax.psum(precise(residual.T, residual), 'dp'))  57.6 us
    dot_general x3, matrix products, contract_rows(): lax.dot_general(left_side, right_side, (((0,), (0,)), ((), ())), preferre...  45.8 us
    reduce_scatter x1, waiting for transfers between devices, per_device(): lax.psum_scatter(contract_rows(activations, member), 'dp', scatter_dimens...  39.5 us
    psum x1, blocking collectives, per_device(): class_weight = lax.psum(local_weight, 'dp')  35 us
    another operation x9, other arithmetic, solve_positive(): jnp.linalg.cholesky(matrix)  19.6 us
  transfers between devices with their start and end apart: 5, of which 5 were waited for; matrix products, arithmetic and copies ran while one was open for 0% of the time, Pallas kernels for 0%

commit v1 on v0

--- a/solution.py
+++ b/solution.py
@@ -6,6 +6,24 @@
 K = 64
 ITERS = 2
 RIDGE = 0.1
+
+
+def ring_gather(shard, axis, dim):
+    ways, here, lap = (lax.axis_size(axis), lax.axis_index(axis), shard.shape[dim])
+    shape = [n * ways if d == dim else n for d, n in enumerate(shard.shape)]
+    full = lax.dynamic_update_slice_in_dim(
+        jnp.zeros(shape, shard.dtype), shard, here * lap, axis=dim
+    )
+    going_up = going_down = shard
+    for far in range(1, ways // 2 + 1):
+        going_up = lax.ppermute(going_up, axis, [(d, (d + 1) % ways) for d in range(ways)])
+        full = lax.dynamic_update_slice_in_dim(full, going_up, (here - far) % ways * lap, axis=dim)
+        if 2 * far < ways:
+            going_down = lax.ppermute(going_down, axis, [(d, (d - 1) % ways) for d in range(ways)])
+            full = lax.dynamic_update_slice_in_dim(
+                full, going_down, (here + far) % ways * lap, axis=dim
+            )
+    return full
 
 
 def precise(left_side, right_side):
@@ -48,7 +66,7 @@
     for iteration in range(ITERS):
         probed = jnp.dot(
             activations,
-            lax.all_gather(direction.astype(jnp.bfloat16), "dp", axis=0, tiled=True),
+            ring_gather(direction.astype(jnp.bfloat16), "dp", 0),
             preferred_element_type=jnp.float32,
         )
         weighted = (weights[:, None] * probed).astype(jnp.bfloat16)

time: 588 us -> 616 us (1.048)
  starting transfers between devices: 0.43 us -> 62.8 us
  waiting for transfers between devices: 260 us -> 228 us
    all_gather x2 -> x0, waiting for transfers between devices: 80.2 us -> none  [per_device(): lax.all_gather(direction.astype(jnp.bfloat16), 'dp', axis=0, tiled=True)]
    ppermute x0 -> x30, starting transfers between devices: none -> 62.7 us  [the longest x14 62.6 us: ring_gather(): lax.ppermute(going_down, axis, [(d, (d - 1) % ways) for d in range(ways)])]
    ppermute x0 -> x30, waiting for transfers between devices: none -> 51.4 us  [the longest x16 51.3 us: ring_gather(): lax.ppermute(going_up, axis, [(d, (d + 1) % ways) for d in range(ways)])]
  transfers between devices with their start and end apart: 5 -> 33, of which waited for: 5 -> 19; matrix products, arithmetic and copies ran while one was open for 0% -> 1% of each run, Pallas kernels for 0% -> 0%
where the time goes in v1:
time: 616 us
  waiting for transfers between devices  228 us (37%)
  blocking collectives  211 us (34%)
  starting transfers between devices  62.8 us (10%)
  matrix products  59.2 us (10%)
  other arithmetic  37.8 us (6%)
  between operations  14.3 us (2%)
    reduce_scatter x2, waiting for transfers between devices, per_device(): lax.psum_scatter(contract_rows(activations, weighted), 'dp', scatter_dime...  138 us
    psum x2, blocking collectives, per_device(): lax.psum((precise(class_means.T, direction), precise(direction.T, panel),...  118 us
    ppermute x14, starting transfers between devices, ring_gather(): lax.ppermute(going_down, axis, [(d, (d - 1) % ways) for d in range(ways)])  62.6 us
    psum x1, blocking collectives, per_device(): renewed = symmetric(lax.psum(precise(residual.T, residual), 'dp'))  57.6 us
    ppermute x16, waiting for transfers between devices, ring_gather(): lax.ppermute(going_up, axis, [(d, (d + 1) % ways) for d in range(ways)])  51.3 us
    dot_general x3, matrix products, contract_rows(): lax.dot_general(left_side, right_side, (((0,), (0,)), ((), ())), preferre...  44.5 us
    reduce_scatter x1, waiting for transfers between devices, per_device(): lax.psum_scatter(contract_rows(activations, member), 'dp', scatter_dimens...  38.9 us
    psum x1, blocking collectives, per_device(): class_weight = lax.psum(local_weight, 'dp')  35 us
  transfers between devices with their start and end apart: 33, of which 19 were waited for; matrix products, arithmetic and copies ran while one was open for 1% of the time, Pallas kernels for 0%

profile of v1, /device:TPU:0, one launch (start us, length us, event | category | flops | bytes accessed | tf_op | source)
XLA Modules:
  0.0 615.6 jit_solution(14897720237163149309)
XLA Ops:
  7.2 0.7 convert_element_type.20
  7.9 8.9 %convolution_bitcast_fusion.2 = f32[16384,64]{0,1:T(8,128)} fusion(bf16[384,16384]{1,0:T(8,128)(2,1)} %param.6, f32[384]{0:T(512)S(1)} %convert_element_type.20, s32[384]{0:T(512)} %param.7), kind=kOutput, calls=%fused_computation.2 | convolution fusion | flops 805355520 | bytes 16780288 | tf_op jit(solution)/shard_map/dot_general | solution.py:44
  16.8 0.6 copy-done.1
  17.5 35.0 %psum.59 = f32[64]{0:T(128)S(1)} all-reduce(f32[64]{0:T(128)S(1)} %select_reduce_fusion), channel_id=1, replica_groups=mesh['groups'=2,'dp'=16] {'dp'}, use_global_device_ids=true, to_apply=%region_2.3 | all-reduce | flops 64 | bytes 512 | tf_op jit(solution)/shard_map/psum | solution.py:58
  52.6 0.6 fusion.62
  53.2 38.9 %reduce-scatter.4.cloned.1.call-done = f32[1024,64]{0,1:T(8,128)} async-done(((f32[16384,64]{0,1:T(8,128)}), f32[1024,64]{0,1:T(8,128)}) %reduce-scatter.4.cloned.1.call-update) | async-done | bytes 262160 | tf_op jit(solution)/shard_map/reduce_scatter | solution.py:55
  92.2 0.8 copy-done
  93.2 4.4 collective-permute-start.1
  97.6 2.6 collective-permute-done
  100.3 4.5 collective-permute-start.3
  104.9 2.6 collective-permute-done.2
  107.5 4.4 collective-permute-start.5
  111.9 2.7 collective-permute-done.4
  114.7 4.4 collective-permute-start.7
  119.1 2.7 collective-permute-done.6
  121.9 4.4 collective-permute-start.9
  126.3 2.7 collective-permute-done.8
  129.1 4.4 collective-permute-start.11
  133.5 2.7 collective-permute-done.10
  136.3 4.4 collective-permute-start.13
  140.7 2.6 collective-permute-done.12
  143.4 7.0 %collective-permute-done.14 = bf16[1024,64]{0,1:T(8,128)(2,1)S(1)} collective-permute-done((bf16[1024,64]{0,1:T(8,128)(2,1)S(1)}, bf16[1024,64]{0,1:T(8,128)(2,1)S(1)}, u32[]{:S(2)}, u32[]{:S(2)}) %collective-permute-start.14) | collective-permute-done | bytes 131104 | tf_op jit(solution)/shard_map/ppermute | solution.py:19
  150.4 17.8 %convolution_bitcast_fusion.1 = f32[16384,64]{0,1:T(8,128)} fusion(bf16[384,16384]{1,0:T(8,128)(2,1)} %param.6, bf16[16384,64]{0,1:T(8,128)(2,1)S(1)} %constant_dynamic-update-slice_fusion.16, f32[384]{0:T(512)S(1)} %convert_element_type.20), kind=kOutput, calls=%fused_computation.1 | convolution fusion | flops 1610661888 | bytes 18875904 | tf_op jit(solution)/shard_map/dot_general | solution.py:44
  169.3 68.7 %reduce-scatter.6.cloned.1.call-done = f32[1024,64]{0,1:T(8,128)} async-done(((f32[16384,64]{0,1:T(8,128)}), f32[1024,64]{0,1:T(8,128)}) %reduce-scatter.6.cloned.1.call-update) | async-done | bytes 262160 | tf_op jit(solution)/shard_map/reduce_scatter | solution.py:73
  238.0 1.4 fusion.17
  239.5 59.2 %all-reduce.1 = (f32[64,64]{1,0:T(8,128)S(1)}, f32[64,64]{1,0:T(8,128)S(1)}, f32[64,64]{1,0:T(8,128)S(1)}) all-reduce(f32[64,64]{1,0:T(8,128)S(1)} %fusion.13, f32[64,64]{1,0:T(8,128)S(1)} %fusion.17, f32[64,64]{1,0:T(8,128)S(1)} %fusion.15), channel_id=1, replica_groups=mesh['groups'=2,'dp'=16] {'dp'}, use_global_device_ids=true, to_apply=%region_7.8 | all-reduce | flops 12288 | bytes 98304 | tf_op jit(solution)/shard_map/psum | solution.py:76
  298.8 5.8 cholesky.70
  304.7 0.6 compare_reduce_fusion.1
  305.4 0.7 fusion.32
  306.0 4.9 custom-call.10
  310.9 0.9 fusion.9
  312.1 5.9 cholesky.59
  318.0 0.6 compare_reduce_fusion.2
  318.7 0.7 fusion.31
  319.3 4.9 custom-call.9
  324.6 1.2 fusion.3
  326.6 57.6 %psum.63 = f32[64,64]{1,0:T(8,128)S(1)} all-reduce(f32[64,64]{1,0:T(8,128)S(1)} %fusion.63), channel_id=1, replica_groups=mesh['groups'=2,'dp'=16] {'dp'}, use_global_device_ids=true, to_apply=%region_10.13 | all-reduce | flops 4096 | bytes 32768 | tf_op jit(solution)/shard_map/psum | solution.py:94
  385.4 4.4 collective-permute-start.16
  389.8 2.8 collective-permute-done.15
  392.6 4.5 collective-permute-start.18
  397.1 2.7 collective-permute-done.17
  399.8 4.5 collective-permute-start.20
  404.3 2.7 collective-permute-done.19
  407.0 4.5 collective-permute-start.22
  411.5 2.7 collective-permute-done.21
  414.2 4.5 collective-permute-start.24
  418.7 2.7 collective-permute-done.23
  421.4 4.5 collective-permute-start.26
  425.9 2.7 collective-permute-done.25
  428.6 4.5 collective-permute-start.28
  433.1 2.5 collective-permute-done.27
  435.7 7.0 %collective-permute-done.29 = bf16[1024,64]{0,1:T(8,128)(2,1)S(1)} collective-permute-done((bf16[1024,64]{0,1:T(8,128)(2,1)S(1)}, bf16[1024,64]{0,1:T(8,128)(2,1)S(1)}, u32[]{:S(2)}, u32[]{:S(2)}) %collective-permute-start.29) | collective-permute-done | bytes 131104 | tf_op jit(solution)/shard_map/ppermute | solution.py:19
  442.8 17.8 %convolution_bitcast_fusion = f32[16384,64]{0,1:T(8,128)} fusion(bf16[384,16384]{1,0:T(8,128)(2,1)} %param.6, bf16[16384,64]{0,1:T(8,128)(2,1)S(1)} %constant_dynamic-update-slice_fusion, f32[384]{0:T(512)S(1)} %convert_element_type.20), kind=kOutput, calls=%fused_computation | convolution fusion | flops 1610661888 | bytes 18875904 | tf_op jit(solution)/shard_map/dot_general | solution.py:44
  461.9 68.8 %reduce-scatter.8.cloned.1.call-done = f32[1024,64]{0,1:T(8,128)} async-done(((f32[16384,64]{0,1:T(8,128)}), f32[1024,64]{0,1:T(8,128)}) %reduce-scatter.8.cloned.1.call-update) | async-done | bytes 262160 | tf_op jit(solution)/shard_map/reduce_scatter | solution.py:73
  530.7 1.3 fusion.64
  532.0 59.1 %all-reduce = (f32[64,64]{1,0:T(8,128)S(1)}, f32[64,64]{1,0:T(8,128)S(1)}, f32[64,64]{1,0:T(8,128)S(1)}) all-reduce(f32[64,64]{1,0:T(8,128)S(1)} %fusion.64, f32[64,64]{1,0:T(8,128)S(1)} %fusion.61, f32[64,64]{1,0:T(8,128)S(1)} %fusion.65), channel_id=1, replica_groups=mesh['groups'=2,'dp'=16] {'dp'}, use_global_device_ids=true, to_apply=%region_12.15 | all-reduce | flops 12288 | bytes 98304 | tf_op jit(solution)/shard_map/psum | solution.py:76
  591.0 0.9 fusion.7
  592.2 5.8 cholesky.81
  598.1 0.6 compare_reduce_fusion
  598.8 0.7 fusion.33
  599.4 4.9 custom-call.11
  604.7 2.1 fusion.1
  606.9 1.1 convolution_subtract_fusion
  608.0 1.1 convolution_add_fusion
  (107 shorter events, 6.7 us)
Async XLA Ops:
  7.2 84.9 %reduce-scatter.4.cloned.1.call-start = ((), (), s32[]{:S(2)}) async-start(), calls=%async_computation.3 | async-start | bytes 4456448 | tf_op jit(solution)/shard_map/reduce_scatter | solution.py:55
  16.8 0.7 copy-start.1
  16.8 221.2 %reduce-scatter.6.cloned.1.call-start = ((), (), s32[]{:S(2)}) async-start(), calls=%async_computation.4 | async-start | bytes 4456448 | tf_op jit(solution)/shard_map/reduce_scatter | solution.py:73
  92.1 0.9 copy-start
  93.1 7.1 %collective-permute-start = (bf16[1024,64]{0,1:T(8,128)(2,1)S(1)}, bf16[1024,64]{0,1:T(8,128)(2,1)S(1)}, u32[]{:S(2)}, u32[]{:S(2)}) collective-permute-start(bf16[1024,64]{0,1:T(8,128)(2,1)S(1)} %get-tuple-element.13), channel_id=1, source_target_pairs={{0,1},{1,2},{2,3},{3,4},{4,5},{5,6},{6,7},{7,8},{8,9},{9,10},{10,1... | collective-permute-start | bytes 393224 | tf_op jit(solution)/shard_map/ppermute | solution.py:19
  93.2 7.1 %collective-permute-start.1 = (bf16[1024,64]{0,1:T(8,128)(2,1)S(1)}, bf16[1024,64]{0,1:T(8,128)(2,1)S(1)}, u32[]{:S(2)}, u32[]{:S(2)}) collective-permute-start(bf16[1024,64]{0,1:T(8,128)(2,1)S(1)} %get-tuple-element.13), channel_id=1, source_target_pairs={{0,15},{1,0},{2,1},{3,2},{4,3},{5,4},{6,5},{7,6},{8,7},{9,8},{10,9... | collective-permute-start | bytes 393224 | tf_op jit(solution)/shard_map/ppermute | solution.py:22
  100.3 7.2 %collective-permute-start.2 = (bf16[1024,64]{0,1:T(8,128)(2,1)S(1)}, bf16[1024,64]{0,1:T(8,128)(2,1)S(1)}, u32[]{:S(2)}, u32[]{:S(2)}) collective-permute-start(bf16[1024,64]{0,1:T(8,128)(2,1)S(1)} %collective-permute-done), channel_id=1, source_target_pairs={{0,1},{1,2},{2,3},{3,4},{4,5},{5,6},{6,7},{7,8},{8,9},{9,10},{10,1... | collective-permute-start | bytes 393224 | tf_op jit(solution)/shard_map/ppermute | solution.py:19
  100.3 7.2 %collective-permute-start.3 = (bf16[1024,64]{0,1:T(8,128)(2,1)S(1)}, bf16[1024,64]{0,1:T(8,128)(2,1)S(1)}, u32[]{:S(2)}, u32[]{:S(2)}) collective-permute-start(bf16[1024,64]{0,1:T(8,128)(2,1)S(1)} %collective-permute-done.1), channel_id=1, source_target_pairs={{0,15},{1,0},{2,1},{3,2},{4,3},{5,4},{6,5},{7,6},{8,7},{9,8},{10,9... | collective-permute-start | bytes 393224 | tf_op jit(solution)/shard_map/ppermute | solution.py:22
  107.5 7.2 %collective-permute-start.4 = (bf16[1024,64]{0,1:T(8,128)(2,1)S(1)}, bf16[1024,64]{0,1:T(8,128)(2,1)S(1)}, u32[]{:S(2)}, u32[]{:S(2)}) collective-permute-start(bf16[1024,64]{0,1:T(8,128)(2,1)S(1)} %collective-permute-done.2), channel_id=1, source_target_pairs={{0,1},{1,2},{2,3},{3,4},{4,5},{5,6},{6,7},{7,8},{8,9},{9,10},{10,1... | collective-permute-start | bytes 393224 | tf_op jit(solution)/shard_map/ppermute | solution.py:19
  107.5 7.2 %collective-permute-start.5 = (bf16[1024,64]{0,1:T(8,128)(2,1)S(1)}, bf16[1024,64]{0,1:T(8,128)(2,1)S(1)}, u32[]{:S(2)}, u32[]{:S(2)}) collective-permute-start(bf16[1024,64]{0,1:T(8,128)(2,1)S(1)} %collective-permute-done.3), channel_id=1, source_target_pairs={{0,15},{1,0},{2,1},{3,2},{4,3},{5,4},{6,5},{7,6},{8,7},{9,8},{10,9... | collective-permute-start | bytes 393224 | tf_op jit(solution)/shard_map/ppermute | solution.py:22
  114.7 7.2 %collective-permute-start.6 = (bf16[1024,64]{0,1:T(8,128)(2,1)S(1)}, bf16[1024,64]{0,1:T(8,128)(2,1)S(1)}, u32[]{:S(2)}, u32[]{:S(2)}) collective-permute-start(bf16[1024,64]{0,1:T(8,128)(2,1)S(1)} %collective-permute-done.4), channel_id=1, source_target_pairs={{0,1},{1,2},{2,3},{3,4},{4,5},{5,6},{6,7},{7,8},{8,9},{9,10},{10,1... | collective-permute-start | bytes 393224 | tf_op jit(solution)/shard_map/ppermute | solution.py:19
  114.7 7.2 %collective-permute-start.7 = (bf16[1024,64]{0,1:T(8,128)(2,1)S(1)}, bf16[1024,64]{0,1:T(8,128)(2,1)S(1)}, u32[]{:S(2)}, u32[]{:S(2)}) collective-permute-start(bf16[1024,64]{0,1:T(8,128)(2,1)S(1)} %collective-permute-done.5), channel_id=1, source_target_pairs={{0,15},{1,0},{2,1},{3,2},{4,3},{5,4},{6,5},{7,6},{8,7},{9,8},{10,9... | collective-permute-start | bytes 393224 | tf_op jit(solution)/shard_map/ppermute | solution.py:22
  121.9 7.2 %collective-permute-start.8 = (bf16[1024,64]{0,1:T(8,128)(2,1)S(1)}, bf16[1024,64]{0,1:T(8,128)(2,1)S(1)}, u32[]{:S(2)}, u32[]{:S(2)}) collective-permute-start(bf16[1024,64]{0,1:T(8,128)(2,1)S(1)} %collective-permute-done.6), channel_id=1, source_target_pairs={{0,1},{1,2},{2,3},{3,4},{4,5},{5,6},{6,7},{7,8},{8,9},{9,10},{10,1... | collective-permute-start | bytes 393224 | tf_op jit(solution)/shard_map/ppermute | solution.py:19
  121.9 7.2 %collective-permute-start.9 = (bf16[1024,64]{0,1:T(8,128)(2,1)S(1)}, bf16[1024,64]{0,1:T(8,128)(2,1)S(1)}, u32[]{:S(2)}, u32[]{:S(2)}) collective-permute-start(bf16[1024,64]{0,1:T(8,128)(2,1)S(1)} %collective-permute-done.7), channel_id=1, source_target_pairs={{0,15},{1,0},{2,1},{3,2},{4,3},{5,4},{6,5},{7,6},{8,7},{9,8},{10,9... | collective-permute-start | bytes 393224 | tf_op jit(solution)/shard_map/ppermute | solution.py:22
  129.1 7.2 %collective-permute-start.10 = (bf16[1024,64]{0,1:T(8,128)(2,1)S(1)}, bf16[1024,64]{0,1:T(8,128)(2,1)S(1)}, u32[]{:S(2)}, u32[]{:S(2)}) collective-permute-start(bf16[1024,64]{0,1:T(8,128)(2,1)S(1)} %collective-permute-done.8), channel_id=1, source_target_pairs={{0,1},{1,2},{2,3},{3,4},{4,5},{5,6},{6,7},{7,8},{8,9},{9,10},{10,1... | collective-permute-start | bytes 393224 | tf_op jit(solution)/shard_map/ppermute | solution.py:19
  129.1 7.2 %collective-permute-start.11 = (bf16[1024,64]{0,1:T(8,128)(2,1)S(1)}, bf16[1024,64]{0,1:T(8,128)(2,1)S(1)}, u32[]{:S(2)}, u32[]{:S(2)}) collective-permute-start(bf16[1024,64]{0,1:T(8,128)(2,1)S(1)} %collective-permute-done.9), channel_id=1, source_target_pairs={{0,15},{1,0},{2,1},{3,2},{4,3},{5,4},{6,5},{7,6},{8,7},{9,8},{10,9... | collective-permute-start | bytes 393224 | tf_op jit(solution)/shard_map/ppermute | solution.py:22
  136.3 7.1 %collective-permute-start.12 = (bf16[1024,64]{0,1:T(8,128)(2,1)S(1)}, bf16[1024,64]{0,1:T(8,128)(2,1)S(1)}, u32[]{:S(2)}, u32[]{:S(2)}) collective-permute-start(bf16[1024,64]{0,1:T(8,128)(2,1)S(1)} %collective-permute-done.10), channel_id=1, source_target_pairs={{0,1},{1,2},{2,3},{3,4},{4,5},{5,6},{6,7},{7,8},{8,9},{9,10},{10,1... | collective-permute-start | bytes 393224 | tf_op jit(solution)/shard_map/ppermute | solution.py:19
  136.3 7.1 %collective-permute-start.13 = (bf16[1024,64]{0,1:T(8,128)(2,1)S(1)}, bf16[1024,64]{0,1:T(8,128)(2,1)S(1)}, u32[]{:S(2)}, u32[]{:S(2)}) collective-permute-start(bf16[1024,64]{0,1:T(8,128)(2,1)S(1)} %collective-permute-done.11), channel_id=1, source_target_pairs={{0,15},{1,0},{2,1},{3,2},{4,3},{5,4},{6,5},{7,6},{8,7},{9,8},{10,9... | collective-permute-start | bytes 393224 | tf_op jit(solution)/shard_map/ppermute | solution.py:22
  143.3 7.1 %collective-permute-start.14 = (bf16[1024,64]{0,1:T(8,128)(2,1)S(1)}, bf16[1024,64]{0,1:T(8,128)(2,1)S(1)}, u32[]{:S(2)}, u32[]{:S(2)}) collective-permute-start(bf16[1024,64]{0,1:T(8,128)(2,1)S(1)} %collective-permute-done.12), channel_id=1, source_target_pairs={{0,1},{1,2},{2,3},{3,4},{4,5},{5,6},{6,7},{7,8},{8,9},{9,10},{10,1... | collective-permute-start | bytes 393224 | tf_op jit(solution)/shard_map/ppermute | solution.py:19
  168.3 362.4 %reduce-scatter.8.cloned.1.call-start = ((), (), s32[]{:S(2)}) async-start(), calls=%async_computation.5 | async-start | bytes 4456448 | tf_op jit(solution)/shard_map/reduce_scatter | solution.py:73
  238.0 86.6 %copy-start.2 = (f32[1024,64]{0,1:T(8,128)S(1)}, f32[1024,64]{0,1:T(8,128)}, u32[]{:S(2)}) copy-start(f32[1024,64]{0,1:T(8,128)} %reduce-scatter.6.cloned.1.call-done) | copy-start | bytes 786436
  385.3 7.2 %collective-permute-start.15 = (bf16[1024,64]{0,1:T(8,128)(2,1)S(1)}, bf16[1024,64]{0,1:T(8,128)(2,1)S(1)}, u32[]{:S(2)}, u32[]{:S(2)}) collective-permute-start(bf16[1024,64]{0,1:T(8,128)(2,1)S(1)} %get-tuple-element.11), channel_id=1, source_target_pairs={{0,1},{1,2},{2,3},{3,4},{4,5},{5,6},{6,7},{7,8},{8,9},{9,10},{10,1... | collective-permute-start | bytes 393224 | tf_op jit(solution)/shard_map/ppermute | solution.py:19
  385.4 7.2 %collective-permute-start.16 = (bf16[1024,64]{0,1:T(8,128)(2,1)S(1)}, bf16[1024,64]{0,1:T(8,128)(2,1)S(1)}, u32[]{:S(2)}, u32[]{:S(2)}) collective-permute-start(bf16[1024,64]{0,1:T(8,128)(2,1)S(1)} %get-tuple-element.11), channel_id=1, source_target_pairs={{0,15},{1,0},{2,1},{3,2},{4,3},{5,4},{6,5},{7,6},{8,7},{9,8},{10,9... | collective-permute-start | bytes 393224 | tf_op jit(solution)/shard_map/ppermute | solution.py:22
  392.6 7.2 %collective-permute-start.17 = (bf16[1024,64]{0,1:T(8,128)(2,1)S(1)}, bf16[1024,64]{0,1:T(8,128)(2,1)S(1)}, u32[]{:S(2)}, u32[]{:S(2)}) collective-permute-start(bf16[1024,64]{0,1:T(8,128)(2,1)S(1)} %collective-permute-done.15), channel_id=1, source_target_pairs={{0,1},{1,2},{2,3},{3,4},{4,5},{5,6},{6,7},{7,8},{8,9},{9,10},{10,1... | collective-permute-start | bytes 393224 | tf_op jit(solution)/shard_map/ppermute | solution.py:19
  392.6 7.2 %collective-permute-start.18 = (bf16[1024,64]{0,1:T(8,128)(2,1)S(1)}, bf16[1024,64]{0,1:T(8,128)(2,1)S(1)}, u32[]{:S(2)}, u32[]{:S(2)}) collective-permute-start(bf16[1024,64]{0,1:T(8,128)(2,1)S(1)} %collective-permute-done.16), channel_id=1, source_target_pairs={{0,15},{1,0},{2,1},{3,2},{4,3},{5,4},{6,5},{7,6},{8,7},{9,8},{10,9... | collective-permute-start | bytes 393224 | tf_op jit(solution)/shard_map/ppermute | solution.py:22
  399.8 7.2 %collective-permute-start.19 = (bf16[1024,64]{0,1:T(8,128)(2,1)S(1)}, bf16[1024,64]{0,1:T(8,128)(2,1)S(1)}, u32[]{:S(2)}, u32[]{:S(2)}) collective-permute-start(bf16[1024,64]{0,1:T(8,128)(2,1)S(1)} %collective-permute-done.17), channel_id=1, source_target_pairs={{0,1},{1,2},{2,3},{3,4},{4,5},{5,6},{6,7},{7,8},{8,9},{9,10},{10,1... | collective-permute-start | bytes 393224 | tf_op jit(solution)/shard_map/ppermute | solution.py:19
  399.8 7.2 %collective-permute-start.20 = (bf16[1024,64]{0,1:T(8,128)(2,1)S(1)}, bf16[1024,64]{0,1:T(8,128)(2,1)S(1)}, u32[]{:S(2)}, u32[]{:S(2)}) collective-permute-start(bf16[1024,64]{0,1:T(8,128)(2,1)S(1)} %collective-permute-done.18), channel_id=1, source_target_pairs={{0,15},{1,0},{2,1},{3,2},{4,3},{5,4},{6,5},{7,6},{8,7},{9,8},{10,9... | collective-permute-start | bytes 393224 | tf_op jit(solution)/shard_map/ppermute | solution.py:22
  407.0 7.2 %collective-permute-start.21 = (bf16[1024,64]{0,1:T(8,128)(2,1)S(1)}, bf16[1024,64]{0,1:T(8,128)(2,1)S(1)}, u32[]{:S(2)}, u32[]{:S(2)}) collective-permute-start(bf16[1024,64]{0,1:T(8,128)(2,1)S(1)} %collective-permute-done.19), channel_id=1, source_target_pairs={{0,1},{1,2},{2,3},{3,4},{4,5},{5,6},{6,7},{7,8},{8,9},{9,10},{10,1... | collective-permute-start | bytes 393224 | tf_op jit(solution)/shard_map/ppermute | solution.py:19
  407.0 7.2 %collective-permute-start.22 = (bf16[1024,64]{0,1:T(8,128)(2,1)S(1)}, bf16[1024,64]{0,1:T(8,128)(2,1)S(1)}, u32[]{:S(2)}, u32[]{:S(2)}) collective-permute-start(bf16[1024,64]{0,1:T(8,128)(2,1)S(1)} %collective-permute-done.20), channel_id=1, source_target_pairs={{0,15},{1,0},{2,1},{3,2},{4,3},{5,4},{6,5},{7,6},{8,7},{9,8},{10,9... | collective-permute-start | bytes 393224 | tf_op jit(solution)/shard_map/ppermute | solution.py:22
  414.2 7.2 %collective-permute-start.23 = (bf16[1024,64]{0,1:T(8,128)(2,1)S(1)}, bf16[1024,64]{0,1:T(8,128)(2,1)S(1)}, u32[]{:S(2)}, u32[]{:S(2)}) collective-permute-start(bf16[1024,64]{0,1:T(8,128)(2,1)S(1)} %collective-permute-done.21), channel_id=1, source_target_pairs={{0,1},{1,2},{2,3},{3,4},{4,5},{5,6},{6,7},{7,8},{8,9},{9,10},{10,1... | collective-permute-start | bytes 393224 | tf_op jit(solution)/shard_map/ppermute | solution.py:19
  414.2 7.2 %collective-permute-start.24 = (bf16[1024,64]{0,1:T(8,128)(2,1)S(1)}, bf16[1024,64]{0,1:T(8,128)(2,1)S(1)}, u32[]{:S(2)}, u32[]{:S(2)}) collective-permute-start(bf16[1024,64]{0,1:T(8,128)(2,1)S(1)} %collective-permute-done.22), channel_id=1, source_target_pairs={{0,15},{1,0},{2,1},{3,2},{4,3},{5,4},{6,5},{7,6},{8,7},{9,8},{10,9... | collective-permute-start | bytes 393224 | tf_op jit(solution)/shard_map/ppermute | solution.py:22
  421.4 7.2 %collective-permute-start.25 = (bf16[1024,64]{0,1:T(8,128)(2,1)S(1)}, bf16[1024,64]{0,1:T(8,128)(2,1)S(1)}, u32[]{:S(2)}, u32[]{:S(2)}) collective-permute-start(bf16[1024,64]{0,1:T(8,128)(2,1)S(1)} %collective-permute-done.23), channel_id=1, source_target_pairs={{0,1},{1,2},{2,3},{3,4},{4,5},{5,6},{6,7},{7,8},{8,9},{9,10},{10,1... | collective-permute-start | bytes 393224 | tf_op jit(solution)/shard_map/ppermute | solution.py:19
  421.4 7.2 %collective-permute-start.26 = (bf16[1024,64]{0,1:T(8,128)(2,1)S(1)}, bf16[1024,64]{0,1:T(8,128)(2,1)S(1)}, u32[]{:S(2)}, u32[]{:S(2)}) collective-permute-start(bf16[1024,64]{0,1:T(8,128)(2,1)S(1)} %collective-permute-done.24), channel_id=1, source_target_pairs={{0,15},{1,0},{2,1},{3,2},{4,3},{5,4},{6,5},{7,6},{8,7},{9,8},{10,9... | collective-permute-start | bytes 393224 | tf_op jit(solution)/shard_map/ppermute | solution.py:22
  428.6 7.1 %collective-permute-start.27 = (bf16[1024,64]{0,1:T(8,128)(2,1)S(1)}, bf16[1024,64]{0,1:T(8,128)(2,1)S(1)}, u32[]{:S(2)}, u32[]{:S(2)}) collective-permute-start(bf16[1024,64]{0,1:T(8,128)(2,1)S(1)} %collective-permute-done.25), channel_id=1, source_target_pairs={{0,1},{1,2},{2,3},{3,4},{4,5},{5,6},{6,7},{7,8},{8,9},{9,10},{10,1... | collective-permute-start | bytes 393224 | tf_op jit(solution)/shard_map/ppermute | solution.py:19
  428.6 7.1 %collective-permute-start.28 = (bf16[1024,64]{0,1:T(8,128)(2,1)S(1)}, bf16[1024,64]{0,1:T(8,128)(2,1)S(1)}, u32[]{:S(2)}, u32[]{:S(2)}) collective-permute-start(bf16[1024,64]{0,1:T(8,128)(2,1)S(1)} %collective-permute-done.26), channel_id=1, source_target_pairs={{0,15},{1,0},{2,1},{3,2},{4,3},{5,4},{6,5},{7,6},{8,7},{9,8},{10,9... | collective-permute-start | bytes 393224 | tf_op jit(solution)/shard_map/ppermute | solution.py:22
  435.7 7.1 %collective-permute-start.29 = (bf16[1024,64]{0,1:T(8,128)(2,1)S(1)}, bf16[1024,64]{0,1:T(8,128)(2,1)S(1)}, u32[]{:S(2)}, u32[]{:S(2)}) collective-permute-start(bf16[1024,64]{0,1:T(8,128)(2,1)S(1)} %collective-permute-done.27), channel_id=1, source_target_pairs={{0,1},{1,2},{2,3},{3,4},{4,5},{5,6},{6,7},{7,8},{8,9},{9,10},{10,1... | collective-permute-start | bytes 393224 | tf_op jit(solution)/shard_map/ppermute | solution.py:19
Sparse Core Ops, SparseCore 0:
  16.9 75.1 reduce-scatter.3
  168.4 69.5 reduce-scatter.5
  460.7 69.8 reduce-scatter.7
